TPU v7x, 256 devices: a whole 4x4x8 slice. The times are simulated.
256 devices in a mesh: seq: 128 (over x, z, y_lo, core), head: 2 (over y_hi).
Axes of the slice: x: 4, y: 4 (y_hi: 2, y_lo: 2; y = y_hi * 2 + y_lo), z: 8, core: 2. Of those that a mesh axis runs over, the one named last changes fastest.
Arguments:
- queries: bfloat16 [1, 32768, 16, 128], P(None, 'seq', 'head'), may hold values from -6 to 6
- keys: bfloat16 [1, 32768, 4, 128], P(None, 'seq', 'head'), may hold values from -6 to 6
- values: bfloat16 [1, 32768, 4, 128], P(None, 'seq', 'head'), may hold values from -6 to 6
- norm_gain: float32 [16, 128], P('head'), may hold values from 0.25 to 1.75
- out_grad: bfloat16 [1, 32768, 16, 128], P(None, 'seq', 'head'), may hold values from -6 to 6
- window_reach: int32 [1, 128], P(None, 'seq'), may hold values from 0 to 256
- partner_mask: int32 [1, 128, 6], P(None, 'seq'), may hold values 0 or 1
Outputs:
- normed: bfloat16 [1, 32768, 16, 128], P(None, 'seq', 'head')
- query_grad: bfloat16 [1, 32768, 16, 128], P(None, 'seq', 'head')
- key_gradient: bfloat16 [1, 32768, 4, 128], P(None, 'seq', 'head')
- value_gradient: bfloat16 [1, 32768, 4, 128], P(None, 'seq', 'head')
All inputs are finite; a program needn't handle non-finite values. No bound on the sum of `partner_mask` on one device may be relied on, other than what follows from the above.
Results may differ from a plain program's by a relative error of at most 0.029.
Values may be sent and summed in bfloat16 or wider, within the bound.
No kernel may reach another device: no remote copies, remote signals or barrier semaphores. Data moves between devices by JAX's collectives and lax.ppermute only.
A program may use at most 64 MiB of HBM per device.

v0:
```python
import math
import jax
import jax.numpy as jnp
from jax import lax
from jax.sharding import PartitionSpec as P

epsilon = 1e-06


def passed_along(value, axis, steps):
    count = lax.axis_size(axis)
    leading, last = (max(0, -steps), min(count, count - steps))
    return lax.ppermute(value, axis, [(source, source + steps) for source in range(leading, last)])


def per_device(queries, keys, values, norm_gain, out_grad, window_reach, partner_mask):
    batch_size, block_rows, local_heads, head_size = queries.shape
    key_heads = keys.shape[2]
    group_size = local_heads // key_heads
    score_scale = 1.0 / math.sqrt(head_size)
    device_count = lax.axis_size("seq")
    my_block = lax.axis_index("seq")
    level_count = len([level for level in range(1, 11) if 2 ** (level + 1) <= device_count])
    grouped = queries.reshape(batch_size, block_rows, key_heads, group_size, head_size)
    window_pair = passed_along((keys, values), "seq", 1)
    partner_pairs = []
    for level in range(1, level_count + 1):
        partner_pairs.append(passed_along((keys, values), "seq", 2**level))
    query_pos = lax.broadcasted_iota(jnp.int32, (block_rows, block_rows), 0)
    key_pos = lax.broadcasted_iota(jnp.int32, (block_rows, block_rows), 1)
    own_mask = (key_pos <= query_pos)[None, None, None]
    window_mask = (
        (key_pos[None] >= block_rows - window_reach[:, 0][:, None, None]) & (my_block >= 1)
    )[:, None, None]
    block_list = [(keys, values, own_mask), (window_pair[0], window_pair[1], window_mask)]
    for level in range(1, level_count + 1):
        level_on = (partner_mask[:, 0, level - 1] == 1) & (my_block >= 2**level)
        block_list.append(
            (
                partner_pairs[level - 1][0],
                partner_pairs[level - 1][1],
                level_on[:, None, None, None, None],
            )
        )

    def scores_of(key_block, key_mask):
        raw_scores = (
            jnp.einsum("buhgd,bshd->bhgus", grouped, key_block, preferred_element_type=jnp.float32)
            * score_scale
        )
        return jnp.where(key_mask, raw_scores, -jnp.inf)

    score_list = [scores_of(key_block, key_mask) for key_block, value_block, key_mask in block_list]
    running = jnp.max(score_list[0], axis=-1)
    exp_total = jnp.sum(jnp.exp(score_list[0] - running[..., None]), axis=-1)
    for current in score_list[1:]:
        updated = jnp.maximum(running, jnp.max(current, axis=-1))
        exp_total = exp_total * jnp.exp(running - updated) + jnp.sum(
            jnp.exp(current - updated[..., None]), axis=-1
        )
        running = updated
    log_total = running + jnp.log(exp_total)
    weight_list = [jnp.exp(current - log_total[..., None]) for current in score_list]
    prob_list = [weights.astype(jnp.bfloat16) for weights in weight_list]
    accumulated = jnp.zeros(grouped.shape, jnp.float32)
    for entry, probabilities in zip(block_list, prob_list):
        accumulated = accumulated + jnp.einsum(
            "bhgus,bshd->buhgd", probabilities, entry[1], preferred_element_type=jnp.float32
        )
    attention = accumulated.astype(jnp.bfloat16).reshape(
        batch_size, block_rows, local_heads, head_size
    )
    features = local_heads * lax.axis_size("head") * head_size
    attn_wide = attention.astype(jnp.float32)
    square_total = lax.psum(jnp.sum(attn_wide * attn_wide, axis=(2, 3)), "head")
    inverse = lax.rsqrt(square_total / features + epsilon)
    normed = (norm_gain * attn_wide * inverse[..., None, None]).astype(jnp.bfloat16)
    scaled_grad = norm_gain * out_grad.astype(jnp.float32)
    dot_total = lax.psum(jnp.sum(scaled_grad * attn_wide, axis=(2, 3)), "head")
    attention_gradient = (
        scaled_grad * inverse[..., None, None]
        - attn_wide * (dot_total * inverse**3 / features)[..., None, None]
    ).astype(jnp.bfloat16)
    correction_rows = jnp.sum(attention_gradient.astype(jnp.float32) * attn_wide, axis=-1)
    correction_rows = correction_rows.reshape(
        batch_size, block_rows, key_heads, group_size
    ).transpose(0, 2, 3, 1)
    grad_grouped = attention_gradient.reshape(
        batch_size, block_rows, key_heads, group_size, head_size
    )
    query_acc = jnp.zeros(grouped.shape, jnp.float32)
    partials = []
    for entry, weights, probabilities in zip(block_list, weight_list, prob_list):
        key_block, value_block = (entry[0], entry[1])
        prob_grad = jnp.einsum(
            "buhgd,bshd->bhgus", grad_grouped, value_block, preferred_element_type=jnp.float32
        )
        score_grad = (weights * (prob_grad - correction_rows[..., None])).astype(jnp.bfloat16)
        query_acc = query_acc + jnp.einsum(
            "bhgus,bshd->buhgd", score_grad, key_block, preferred_element_type=jnp.float32
        )
        key_part = jnp.einsum(
            "bhgus,buhgd->bshd", score_grad, grouped, preferred_element_type=jnp.float32
        )
        value_part = jnp.einsum(
            "bhgus,buhgd->bshd", probabilities, grad_grouped, preferred_element_type=jnp.float32
        )
        partials.append((key_part, value_part))
    key_sum, value_sum = partials[0]
    nearest = partials[1]
    for level in range(1, level_count + 1):
        level_part = partials[level + 1]
        arrived = (
            passed_along(level_part[0].astype(jnp.bfloat16), "seq", -(2**level)).astype(
                jnp.float32
            ),
            passed_along(level_part[1].astype(jnp.bfloat16), "seq", -(2**level)).astype(
                jnp.float32
            ),
        )
        key_sum = key_sum + arrived[0]
        value_sum = value_sum + arrived[1]
    arrived = (
        passed_along(nearest[0].astype(jnp.bfloat16), "seq", -1).astype(jnp.float32),
        passed_along(nearest[1].astype(jnp.bfloat16), "seq", -1).astype(jnp.float32),
    )
    key_sum = key_sum + arrived[0]
    value_sum = value_sum + arrived[1]
    query_grad = (
        (query_acc * score_scale)
        .astype(jnp.bfloat16)
        .reshape(batch_size, block_rows, local_heads, head_size)
    )
    key_gradient = (key_sum * score_scale).astype(jnp.bfloat16)
    value_gradient = value_sum.astype(jnp.bfloat16)
    return (normed, query_grad, key_gradient, value_gradient)


def solution(mesh):
    return jax.shard_map(
        per_device,
        mesh=mesh,
        in_specs=(
            P(None, "seq", "head", None),
            P(None, "seq", "head", None),
            P(None, "seq", "head", None),
            P("head", None),
            P(None, "seq", "head", None),
            P(None, "seq"),
            P(None, "seq", None),
        ),
        out_specs=(
            P(None, "seq", "head", None),
            P(None, "seq", "head", None),
            P(None, "seq", "head", None),
            P(None, "seq", "head", None),
        ),
        check_vma=False,
    )
```

profile of v0, /device:TPU:227, one launch (start us, length us, event | category | flops | bytes accessed | tf_op | source)
XLA Modules:
  0.0 215.6 jit_solution(11145276876369639496)
XLA Ops:
  0.7 1.7 copy.222
  2.4 3.7 %collective-permute-start.13 = (bf16[1,256,2,128]{1,3,2,0:T(8,128)(2,1)}, bf16[1,256,2,128]{1,3,2,0:T(8,128)(2,1)S(1)}, u32[]{:S(2)}, u32[]{:S(2)}) collective-permute-start(bf16[1,256,2,128]{1,3,2,0:T(8,128)(2,1)} %copy.222), channel_id=1, source_target_pairs={{0,128},{2,130},{4,132},{6,134},{8,136},{10,138},{12,140},{14,142}... | collective-permute-start | bytes 393224 | tf_op jit(solution)/shard_map/ppermute | solution.py:13
  6.2 1.9 collective-permute-start.12
  8.1 2.4 %collective-permute-start.11 = (bf16[1,256,2,128]{1,3,2,0:T(8,128)(2,1)}, bf16[1,256,2,128]{1,3,2,0:T(8,128)(2,1)S(1)}, u32[]{:S(2)}, u32[]{:S(2)}) collective-permute-start(bf16[1,256,2,128]{1,3,2,0:T(8,128)(2,1)} %copy.222), channel_id=1, source_target_pairs={{0,32},{2,34},{4,36},{6,38},{8,40},{10,42},{12,44},{14,46},{16,48}... | collective-permute-start | bytes 393224 | tf_op jit(solution)/shard_map/ppermute | solution.py:13
  10.5 5.2 %collective-permute-start.10 = (bf16[1,256,2,128]{1,3,2,0:T(8,128)(2,1)}, bf16[1,256,2,128]{1,3,2,0:T(8,128)(2,1)}, u32[]{:S(2)}, u32[]{:S(2)}) collective-permute-start(bf16[1,256,2,128]{1,3,2,0:T(8,128)(2,1)} %copy.222), channel_id=1, source_target_pairs={{0,16},{2,18},{4,20},{6,22},{8,24},{10,26},{12,28},{14,30},{16,32}... | collective-permute-start | bytes 393224 | tf_op jit(solution)/shard_map/ppermute | solution.py:13
  16.7 4.6 %collective-permute-start = (bf16[1,256,2,128]{3,1,2,0:T(8,128)(2,1)S(1)}, bf16[1,256,2,128]{3,1,2,0:T(8,128)(2,1)S(1)}, u32[]{:S(2)}, u32[]{:S(2)}) collective-permute-start(bf16[1,256,2,128]{3,1,2,0:T(8,128)(2,1)S(1)} %copy.206), channel_id=1, source_target_pairs={{0,2},{2,4},{4,6},{6,8},{8,10},{10,12},{12,14},{14,16},{16,18},{18... | collective-permute-start | bytes 393224 | tf_op jit(solution)/shard_map/ppermute | solution.py:13
  21.3 1.4 fusion.182
  28.0 2.5 %collective-permute-start.1 = (bf16[1,256,2,128]{3,1,2,0:T(8,128)(2,1)S(1)}, bf16[1,256,2,128]{3,1,2,0:T(8,128)(2,1)S(1)}, u32[]{:S(2)}, u32[]{:S(2)}) collective-permute-start(bf16[1,256,2,128]{3,1,2,0:T(8,128)(2,1)S(1)} %copy.206), channel_id=1, source_target_pairs={{0,4},{2,6},{4,8},{6,10},{8,12},{10,14},{12,16},{14,18},{16,20},{1... | collective-permute-start | bytes 393224 | tf_op jit(solution)/shard_map/ppermute | solution.py:13
  31.0 4.3 %collective-permute-done.1 = bf16[1,256,2,128]{3,1,2,0:T(8,128)(2,1)S(1)} collective-permute-done((bf16[1,256,2,128]{3,1,2,0:T(8,128)(2,1)S(1)}, bf16[1,256,2,128]{3,1,2,0:T(8,128)(2,1)S(1)}, u32[]{:S(2)}, u32[]{:S(2)}) %collective-permute-start.1) | collective-permute-done | bytes 131104 | tf_op jit(solution)/shard_map/ppermute | solution.py:13
  35.3 4.4 %collective-permute-start.2 = (bf16[1,256,2,128]{3,1,2,0:T(8,128)(2,1)S(1)}, bf16[1,256,2,128]{3,1,2,0:T(8,128)(2,1)S(1)}, u32[]{:S(2)}, u32[]{:S(2)}) collective-permute-start(bf16[1,256,2,128]{3,1,2,0:T(8,128)(2,1)S(1)} %copy.206), channel_id=1, source_target_pairs={{0,8},{2,10},{4,12},{6,14},{8,16},{10,18},{12,20},{14,22},{16,24},... | collective-permute-start | bytes 393224 | tf_op jit(solution)/shard_map/ppermute | solution.py:13
  40.2 2.0 collective-permute-done.2
  42.3 2.9 %collective-permute-start.3 = (bf16[1,256,2,128]{3,1,2,0:T(8,128)(2,1)S(1)}, bf16[1,256,2,128]{3,1,2,0:T(8,128)(2,1)S(1)}, u32[]{:S(2)}, u32[]{:S(2)}) collective-permute-start(bf16[1,256,2,128]{3,1,2,0:T(8,128)(2,1)S(1)} %copy.206), channel_id=1, source_target_pairs={{0,16},{2,18},{4,20},{6,22},{8,24},{10,26},{12,28},{14,30},{16,32}... | collective-permute-start | bytes 393224 | tf_op jit(solution)/shard_map/ppermute | solution.py:13
  45.6 5.1 %collective-permute-done.3 = bf16[1,256,2,128]{3,1,2,0:T(8,128)(2,1)S(1)} collective-permute-done((bf16[1,256,2,128]{3,1,2,0:T(8,128)(2,1)S(1)}, bf16[1,256,2,128]{3,1,2,0:T(8,128)(2,1)S(1)}, u32[]{:S(2)}, u32[]{:S(2)}) %collective-permute-start.3) | collective-permute-done | bytes 131104 | tf_op jit(solution)/shard_map/ppermute | solution.py:13
  50.8 1.9 collective-permute-start.4
  53.2 9.1 %collective-permute-done.4 = bf16[1,256,2,128]{3,1,2,0:T(8,128)(2,1)S(1)} collective-permute-done((bf16[1,256,2,128]{3,1,2,0:T(8,128)(2,1)S(1)}, bf16[1,256,2,128]{3,1,2,0:T(8,128)(2,1)S(1)}, u32[]{:S(2)}, u32[]{:S(2)}) %collective-permute-start.4) | collective-permute-done | bytes 131104 | tf_op jit(solution)/shard_map/ppermute | solution.py:13
  62.3 1.9 collective-permute-start.5
  64.7 3.3 %collective-permute-done.5 = bf16[1,256,2,128]{3,1,2,0:T(8,128)(2,1)S(1)} collective-permute-done((bf16[1,256,2,128]{3,1,2,0:T(8,128)(2,1)S(1)}, bf16[1,256,2,128]{3,1,2,0:T(8,128)(2,1)S(1)}, u32[]{:S(2)}, u32[]{:S(2)}) %collective-permute-start.5) | collective-permute-done | bytes 131104 | tf_op jit(solution)/shard_map/ppermute | solution.py:13
  69.8 1.4 collective-permute-done.6
  71.2 6.7 %collective-permute-start.7 = (bf16[1,256,2,128]{1,3,2,0:T(8,128)(2,1)}, bf16[1,256,2,128]{1,3,2,0:T(8,128)(2,1)S(1)}, u32[]{:S(2)}, u32[]{:S(2)}) collective-permute-start(bf16[1,256,2,128]{1,3,2,0:T(8,128)(2,1)} %copy.222), channel_id=1, source_target_pairs={{0,2},{2,4},{4,6},{6,8},{8,10},{10,12},{12,14},{14,16},{16,18},{18... | collective-permute-start | bytes 393224 | tf_op jit(solution)/shard_map/ppermute | solution.py:13
  81.5 12.9 %collective-permute-start.9 = (bf16[1,256,2,128]{1,3,2,0:T(8,128)(2,1)}, bf16[1,256,2,128]{1,3,2,0:T(8,128)(2,1)S(1)}, u32[]{:S(2)}, u32[]{:S(2)}) collective-permute-start(bf16[1,256,2,128]{1,3,2,0:T(8,128)(2,1)} %copy.222), channel_id=1, source_target_pairs={{0,8},{2,10},{4,12},{6,14},{8,16},{10,18},{12,20},{14,22},{16,24},... | collective-permute-start | bytes 393224 | tf_op jit(solution)/shard_map/ppermute | solution.py:13
  95.0 1.7 collective-permute-done.9
  96.7 4.4 %collective-permute-start.8 = (bf16[1,256,2,128]{1,3,2,0:T(8,128)(2,1)}, bf16[1,256,2,128]{1,3,2,0:T(8,128)(2,1)S(1)}, u32[]{:S(2)}, u32[]{:S(2)}) collective-permute-start(bf16[1,256,2,128]{1,3,2,0:T(8,128)(2,1)} %copy.222), channel_id=1, source_target_pairs={{0,4},{2,6},{4,8},{6,10},{8,12},{10,14},{12,16},{14,18},{16,20},{1... | collective-permute-start | bytes 393224 | tf_op jit(solution)/shard_map/ppermute | solution.py:13
  101.6 1.4 fusion.112
  105.5 1.7 fusion.100
  107.1 2.6 %copy.236 = f32[1,256,8,128]{3,2,1,0:T(8,128)} copy(f32[1,256,8,128]{1,3,2,0:T(8,128)} %bitcast.792) | data formatting | bytes 2097152 | tf_op jit(solution)/shard_map/convert_element_type | solution.py:74
  109.7 2.8 %multiply_reduce_fusion.1 = f32[256]{0:T(256)} fusion(f32[1,256,8,128]{3,2,1,0:T(8,128)} %copy.236, bf16[1,256,8,128]{3,2,1,0:T(8,128)(2,1)S(1)} %copy-done.19, f32[8,128]{1,0:T(8,128)S(1)} %copy-done.53), kind=kLoop, calls=%fused_computation.162 | loop fusion | flops 1048320 | bytes 1577984 | tf_op jit(solution)/shard_map/reduce_sum | solution.py:79
  112.5 5.9 %all-reduce = (f32[1,256]{1,0:T(1,128)}, f32[1,256]{1,0:T(1,128)}) all-reduce(f32[1,256]{1,0:T(1,128)S(1)} %bitcast.830, f32[1,256]{1,0:T(1,128)} %bitcast.833), channel_id=1, replica_groups=mesh['seq'=128,'head'=2] {'head'}, use_global_device_ids=true, to_apply=%region_17.18 | all-reduce | flops 512 | bytes 4096 | tf_op jit(solution)/shard_map/psum | solution.py:75
  119.2 4.0 %multiply_reduce_fusion = (f32[256,8]{1,0:T(8,128)}, bf16[1,256,8,128]{3,2,1,0:T(8,128)(2,1)}, bf16[1,256,8,128]{3,2,1,0:T(8,128)(2,1)}) fusion(f32[1,256,8,128]{3,2,1,0:T(8,128)} %copy.236, f32[256]{0:T(256)S(1)} %bitcast.831, f32[256]{0:T(256)S(1)} %bitcast.832, bf16[1,256,8,128]{3,2,1,0:T(8,128)(2,1)S(1)} %copy-done.19, f32[8,128]{1,0:T(8,128)S(1)} %copy-done.53), kind=kLoop, calls=%fused_computation.160 | loop fusion | flops 3143680 | bytes 2635776 | tf_op jit(solution)/shard_map/reduce_sum | solution.py:84
  123.2 1.3 copy.282
  124.6 2.9 %fusion.78 = bf16[1,256,2,128]{1,3,2,0:T(8,128)(2,1)} fusion(bf16[256,2,4,128]{0,3,2,1:T(8,128)(2,1)S(1)} %copy.282, f32[1,2,4,256,256]{3,4,2,1,0:T(8,128)} %copy-done.6, f32[2,4,256]{2,1,0:T(4,128)S(1)} %bitcast.776), kind=kOutput, calls=%fused_computation.136 | convolution fusion | flops 135331840 | bytes 2760704 | tf_op jit(solution)/shard_map/bhgus,buhgd->bshd/dot_general | solution.py:105
  127.5 2.9 %fusion.79 = bf16[1,256,2,128]{1,3,2,0:T(8,128)(2,1)} fusion(bf16[256,2,4,128]{0,3,2,1:T(8,128)(2,1)S(1)} %copy.282, f32[2,256,256,4]{2,1,3,0:T(8,128)} %copy-done.14, f32[2,4,256]{2,1,0:T(4,128)S(1)} %bitcast.777), kind=kOutput, calls=%fused_computation.137 | convolution fusion | flops 135331840 | bytes 2760704 | tf_op jit(solution)/shard_map/bhgus,buhgd->bshd/dot_general | solution.py:105
  135.1 1.6 copy.243
  143.7 1.7 fusion.46
  148.5 2.1 collective-permute-start.14
  150.6 2.8 %collective-permute-start.21 = (bf16[1,256,2,128]{1,3,2,0:T(8,128)(2,1)S(1)}, bf16[1,256,2,128]{1,3,2,0:T(8,128)(2,1)S(1)}, u32[]{:S(2)}, u32[]{:S(2)}) collective-permute-start(bf16[1,256,2,128]{1,3,2,0:T(8,128)(2,1)S(1)} %copy-done.51), channel_id=1, source_target_pairs={{4,0},{6,2},{8,4},{10,6},{12,8},{14,10},{16,12},{18,14},{20,16},{2... | collective-permute-start | bytes 393224 | tf_op jit(solution)/shard_map/ppermute | solution.py:13
  153.3 1.9 collective-permute-start.15
  155.3 1.9 collective-permute-start.22
  157.2 2.1 collective-permute-start.16
  166.9 6.8 %collective-permute-start.17 = (bf16[1,256,2,128]{3,1,2,0:T(8,128)(2,1)S(1)}, bf16[1,256,2,128]{3,1,2,0:T(8,128)(2,1)S(1)}, u32[]{:S(2)}, u32[]{:S(2)}) collective-permute-start(bf16[1,256,2,128]{3,1,2,0:T(8,128)(2,1)S(1)} %fusion.88), channel_id=1, source_target_pairs={{32,0},{34,2},{36,4},{38,6},{40,8},{42,10},{44,12},{46,14},{48,16}... | collective-permute-start | bytes 393224 | tf_op jit(solution)/shard_map/ppermute | solution.py:13
  173.7 1.9 collective-permute-start.18
  177.0 10.1 %collective-permute-start.20 = (bf16[1,256,2,128]{3,1,2,0:T(8,128)(2,1)S(1)}, bf16[1,256,2,128]{3,1,2,0:T(8,128)(2,1)S(1)}, u32[]{:S(2)}, u32[]{:S(2)}) collective-permute-start(bf16[1,256,2,128]{3,1,2,0:T(8,128)(2,1)S(1)} %fusion.85), channel_id=1, source_target_pairs={{2,0},{4,2},{6,4},{8,6},{10,8},{12,10},{14,12},{16,14},{18,16},{20... | collective-permute-start | bytes 393224 | tf_op jit(solution)/shard_map/ppermute | solution.py:13
  187.6 4.1 %collective-permute-start.23 = (bf16[1,256,2,128]{1,3,2,0:T(8,128)(2,1)S(1)}, bf16[1,256,2,128]{1,3,2,0:T(8,128)(2,1)S(1)}, u32[]{:S(2)}, u32[]{:S(2)}) collective-permute-start(bf16[1,256,2,128]{1,3,2,0:T(8,128)(2,1)S(1)} %fusion.82), channel_id=1, source_target_pairs={{16,0},{18,2},{20,4},{22,6},{24,8},{26,10},{28,12},{30,14},{32,16}... | collective-permute-start | bytes 393224 | tf_op jit(solution)/shard_map/ppermute | solution.py:13
  191.7 1.9 collective-permute-start.24
  193.7 1.9 collective-permute-start.25
  196.9 2.2 %collective-permute-start.27 = (bf16[1,256,2,128]{1,3,2,0:T(8,128)(2,1)S(1)}, bf16[1,256,2,128]{1,3,2,0:T(8,128)(2,1)S(1)}, u32[]{:S(2)}, u32[]{:S(2)}) collective-permute-start(bf16[1,256,2,128]{1,3,2,0:T(8,128)(2,1)S(1)} %copy-done.46), channel_id=1, source_target_pairs={{2,0},{4,2},{6,4},{8,6},{10,8},{12,10},{14,12},{16,14},{18,16},{20... | collective-permute-start | bytes 393224 | tf_op jit(solution)/shard_map/ppermute | solution.py:13
  200.9 5.2 %collective-permute-done.24 = bf16[1,256,2,128]{1,3,2,0:T(8,128)(2,1)S(1)} collective-permute-done((bf16[1,256,2,128]{1,3,2,0:T(8,128)(2,1)S(1)}, bf16[1,256,2,128]{1,3,2,0:T(8,128)(2,1)S(1)}, u32[]{:S(2)}, u32[]{:S(2)}) %collective-permute-start.24) | collective-permute-done | bytes 131104 | tf_op jit(solution)/shard_map/ppermute | solution.py:13
  206.2 2.1 collective-permute-done.25
  208.3 5.9 %collective-permute-done.26 = bf16[1,256,2,128]{1,3,2,0:T(8,128)(2,1)S(1)} collective-permute-done((bf16[1,256,2,128]{1,3,2,0:T(8,128)(2,1)S(1)}, bf16[1,256,2,128]{1,3,2,0:T(8,128)(2,1)S(1)}, u32[]{:S(2)}, u32[]{:S(2)}) %collective-permute-start.26) | collective-permute-done | bytes 131104 | tf_op jit(solution)/shard_map/ppermute | solution.py:13
  (187 shorter events, 41.9 us)
Async XLA Ops:
  0.6 20.7 %copy-start = (bf16[1,256,8,128]{3,2,1,0:T(8,128)(2,1)S(1)}, bf16[1,256,8,128]{3,2,1,0:T(8,128)(2,1)}, u32[]{:S(2)}) copy-start(bf16[1,256,8,128]{3,2,1,0:T(8,128)(2,1)} %param.7) | copy-start | bytes 1572868
  0.6 27.1 %copy-start.33 = (bf16[1,256,2,128]{3,2,1,0:T(2,128)(2,1)S(1)}, bf16[1,256,2,128]{3,2,1,0:T(2,128)(2,1)}, u32[]{:S(2)}) copy-start(bf16[1,256,2,128]{3,2,1,0:T(2,128)(2,1)} %param.9) | copy-start | bytes 393220
  0.7 22.1 %copy-start.52 = (s32[1,1,6]{2,1,0:T(1,128)S(1)}, s32[1,1,6]{2,1,0:T(1,128)}, u32[]{:S(2)}) copy-start(s32[1,1,6]{2,1,0:T(1,128)} %param.13) | copy-start | bytes 76
  2.4 101.7 %collective-permute-start.13 = (bf16[1,256,2,128]{1,3,2,0:T(8,128)(2,1)}, bf16[1,256,2,128]{1,3,2,0:T(8,128)(2,1)S(1)}, u32[]{:S(2)}, u32[]{:S(2)}) collective-permute-start(bf16[1,256,2,128]{1,3,2,0:T(8,128)(2,1)} %copy.222), channel_id=1, source_target_pairs={{0,128},{2,130},{4,132},{6,134},{8,136},{10,138},{12,140},{14,142}... | collective-permute-start | bytes 393224 | tf_op jit(solution)/shard_map/ppermute | solution.py:13
  6.2 97.4 %collective-permute-start.12 = (bf16[1,256,2,128]{1,3,2,0:T(8,128)(2,1)}, bf16[1,256,2,128]{1,3,2,0:T(8,128)(2,1)S(1)}, u32[]{:S(2)}, u32[]{:S(2)}) collective-permute-start(bf16[1,256,2,128]{1,3,2,0:T(8,128)(2,1)} %copy.222), channel_id=1, source_target_pairs={{0,64},{2,66},{4,68},{6,70},{8,72},{10,74},{12,76},{14,78},{16,80}... | collective-permute-start | bytes 393224 | tf_op jit(solution)/shard_map/ppermute | solution.py:13
  8.1 94.9 %collective-permute-start.11 = (bf16[1,256,2,128]{1,3,2,0:T(8,128)(2,1)}, bf16[1,256,2,128]{1,3,2,0:T(8,128)(2,1)S(1)}, u32[]{:S(2)}, u32[]{:S(2)}) collective-permute-start(bf16[1,256,2,128]{1,3,2,0:T(8,128)(2,1)} %copy.222), channel_id=1, source_target_pairs={{0,32},{2,34},{4,36},{6,38},{8,40},{10,42},{12,44},{14,46},{16,48}... | collective-permute-start | bytes 393224 | tf_op jit(solution)/shard_map/ppermute | solution.py:13
  10.5 91.1 %collective-permute-start.10 = (bf16[1,256,2,128]{1,3,2,0:T(8,128)(2,1)}, bf16[1,256,2,128]{1,3,2,0:T(8,128)(2,1)}, u32[]{:S(2)}, u32[]{:S(2)}) collective-permute-start(bf16[1,256,2,128]{1,3,2,0:T(8,128)(2,1)} %copy.222), channel_id=1, source_target_pairs={{0,16},{2,18},{4,20},{6,22},{8,24},{10,26},{12,28},{14,30},{16,32}... | collective-permute-start | bytes 393224 | tf_op jit(solution)/shard_map/ppermute | solution.py:13
  16.7 11.3 %collective-permute-start = (bf16[1,256,2,128]{3,1,2,0:T(8,128)(2,1)S(1)}, bf16[1,256,2,128]{3,1,2,0:T(8,128)(2,1)S(1)}, u32[]{:S(2)}, u32[]{:S(2)}) collective-permute-start(bf16[1,256,2,128]{3,1,2,0:T(8,128)(2,1)S(1)} %copy.206), channel_id=1, source_target_pairs={{0,2},{2,4},{4,6},{6,8},{8,10},{10,12},{12,14},{14,16},{16,18},{18... | collective-permute-start | bytes 393224 | tf_op jit(solution)/shard_map/ppermute | solution.py:13
  22.8 55.7 %copy-start.44 = (f32[2,4,256]{2,1,0:T(4,128)}, f32[2,4,256]{2,1,0:T(4,128)S(1)}, u32[]{:S(2)}) copy-start(f32[2,4,256]{2,1,0:T(4,128)S(1)} %get-tuple-element.48) | copy-start | bytes 24580
  28.0 7.3 %collective-permute-start.1 = (bf16[1,256,2,128]{3,1,2,0:T(8,128)(2,1)S(1)}, bf16[1,256,2,128]{3,1,2,0:T(8,128)(2,1)S(1)}, u32[]{:S(2)}, u32[]{:S(2)}) collective-permute-start(bf16[1,256,2,128]{3,1,2,0:T(8,128)(2,1)S(1)} %copy.206), channel_id=1, source_target_pairs={{0,4},{2,6},{4,8},{6,10},{8,12},{10,14},{12,16},{14,18},{16,20},{1... | collective-permute-start | bytes 393224 | tf_op jit(solution)/shard_map/ppermute | solution.py:13
  31.0 63.4 %copy-start.6 = (f32[1,2,4,256,256]{3,4,2,1,0:T(8,128)}, f32[1,2,4,256,256]{3,4,2,1,0:T(8,128)S(1)}, u32[]{:S(2)}) copy-start(f32[1,2,4,256,256]{3,4,2,1,0:T(8,128)S(1)} %get-tuple-element.51) | copy-start | bytes 6291460
  35.3 7.0 %collective-permute-start.2 = (bf16[1,256,2,128]{3,1,2,0:T(8,128)(2,1)S(1)}, bf16[1,256,2,128]{3,1,2,0:T(8,128)(2,1)S(1)}, u32[]{:S(2)}, u32[]{:S(2)}) collective-permute-start(bf16[1,256,2,128]{3,1,2,0:T(8,128)(2,1)S(1)} %copy.206), channel_id=1, source_target_pairs={{0,8},{2,10},{4,12},{6,14},{8,16},{10,18},{12,20},{14,22},{16,24},... | collective-permute-start | bytes 393224 | tf_op jit(solution)/shard_map/ppermute | solution.py:13
  40.2 64.5 %copy-start.16 = (f32[2,256,256,4]{2,1,3,0:T(8,128)}, f32[2,256,256,4]{2,1,3,0:T(8,128)S(1)}, u32[]{:S(2)}) copy-start(f32[2,256,256,4]{2,1,3,0:T(8,128)S(1)} %get-tuple-element.47) | copy-start | bytes 6291460
  42.3 8.5 %collective-permute-start.3 = (bf16[1,256,2,128]{3,1,2,0:T(8,128)(2,1)S(1)}, bf16[1,256,2,128]{3,1,2,0:T(8,128)(2,1)S(1)}, u32[]{:S(2)}, u32[]{:S(2)}) collective-permute-start(bf16[1,256,2,128]{3,1,2,0:T(8,128)(2,1)S(1)} %copy.206), channel_id=1, source_target_pairs={{0,16},{2,18},{4,20},{6,22},{8,24},{10,26},{12,28},{14,30},{16,32}... | collective-permute-start | bytes 393224 | tf_op jit(solution)/shard_map/ppermute | solution.py:13
  45.6 55.4 %copy-start.8 = (f32[2,256,256,4]{2,1,3,0:T(8,128)}, f32[2,256,256,4]{2,1,3,0:T(8,128)S(1)}, u32[]{:S(2)}) copy-start(f32[2,256,256,4]{2,1,3,0:T(8,128)S(1)} %get-tuple-element.45) | copy-start | bytes 6291460
  50.8 13.9 %copy-start.23 = (bf16[1,256,2,128]{3,1,2,0:T(8,128)(2,1)}, bf16[1,256,2,128]{3,1,2,0:T(8,128)(2,1)S(1)}, u32[]{:S(2)}) copy-start(bf16[1,256,2,128]{3,1,2,0:T(8,128)(2,1)S(1)} %collective-permute-done.3) | copy-start | bytes 393220
  50.8 11.5 %collective-permute-start.4 = (bf16[1,256,2,128]{3,1,2,0:T(8,128)(2,1)S(1)}, bf16[1,256,2,128]{3,1,2,0:T(8,128)(2,1)S(1)}, u32[]{:S(2)}, u32[]{:S(2)}) collective-permute-start(bf16[1,256,2,128]{3,1,2,0:T(8,128)(2,1)S(1)} %copy.206), channel_id=1, source_target_pairs={{0,32},{2,34},{4,36},{6,38},{8,40},{10,42},{12,44},{14,46},{16,48}... | collective-permute-start | bytes 393224 | tf_op jit(solution)/shard_map/ppermute | solution.py:13
  53.2 48.4 %copy-start.1 = (f32[2,256,256,4]{2,1,3,0:T(8,128)}, f32[2,256,256,4]{2,1,3,0:T(8,128)S(1)}, u32[]{:S(2)}) copy-start(f32[2,256,256,4]{2,1,3,0:T(8,128)S(1)} %get-tuple-element.43) | copy-start | bytes 6291460
  62.3 5.7 %collective-permute-start.5 = (bf16[1,256,2,128]{3,1,2,0:T(8,128)(2,1)S(1)}, bf16[1,256,2,128]{3,1,2,0:T(8,128)(2,1)S(1)}, u32[]{:S(2)}, u32[]{:S(2)}) collective-permute-start(bf16[1,256,2,128]{3,1,2,0:T(8,128)(2,1)S(1)} %copy.206), channel_id=1, source_target_pairs={{0,64},{2,66},{4,68},{6,70},{8,72},{10,74},{12,76},{14,78},{16,80}... | collective-permute-start | bytes 393224 | tf_op jit(solution)/shard_map/ppermute | solution.py:13
  64.7 38.4 %copy-start.3 = (f32[2,256,256,4]{2,1,3,0:T(8,128)}, f32[2,256,256,4]{2,1,3,0:T(8,128)S(1)}, u32[]{:S(2)}) copy-start(f32[2,256,256,4]{2,1,3,0:T(8,128)S(1)} %get-tuple-element.41) | copy-start | bytes 6291460
  68.0 3.2 %collective-permute-start.6 = (bf16[1,256,2,128]{3,1,2,0:T(8,128)(2,1)S(1)}, bf16[1,256,2,128]{3,1,2,0:T(8,128)(2,1)S(1)}, u32[]{:S(2)}, u32[]{:S(2)}) collective-permute-start(bf16[1,256,2,128]{3,1,2,0:T(8,128)(2,1)S(1)} %copy.206), channel_id=1, source_target_pairs={{0,128},{2,130},{4,132},{6,134},{8,136},{10,138},{12,140},{14,142}... | collective-permute-start | bytes 393224 | tf_op jit(solution)/shard_map/ppermute | solution.py:13
  69.7 33.8 %copy-start.11 = (f32[2,256,256,4]{2,1,3,0:T(8,128)}, f32[2,256,256,4]{2,1,3,0:T(8,128)S(1)}, u32[]{:S(2)}) copy-start(f32[2,256,256,4]{2,1,3,0:T(8,128)S(1)} %get-tuple-element.39) | copy-start | bytes 6291460
  71.2 10.3 %collective-permute-start.7 = (bf16[1,256,2,128]{1,3,2,0:T(8,128)(2,1)}, bf16[1,256,2,128]{1,3,2,0:T(8,128)(2,1)S(1)}, u32[]{:S(2)}, u32[]{:S(2)}) collective-permute-start(bf16[1,256,2,128]{1,3,2,0:T(8,128)(2,1)} %copy.222), channel_id=1, source_target_pairs={{0,2},{2,4},{4,6},{6,8},{8,10},{10,12},{12,14},{14,16},{16,18},{18... | collective-permute-start | bytes 393224 | tf_op jit(solution)/shard_map/ppermute | solution.py:13
  78.4 25.7 %copy-start.14 = (f32[2,256,256,4]{2,1,3,0:T(8,128)}, f32[2,256,256,4]{2,1,3,0:T(8,128)S(1)}, u32[]{:S(2)}) copy-start(f32[2,256,256,4]{2,1,3,0:T(8,128)S(1)} %get-tuple-element.37) | copy-start | bytes 6291460
  81.5 13.5 %copy-start.40 = (bf16[1,256,2,128]{1,3,2,0:T(8,128)(2,1)}, bf16[1,256,2,128]{1,3,2,0:T(8,128)(2,1)S(1)}, u32[]{:S(2)}) copy-start(bf16[1,256,2,128]{1,3,2,0:T(8,128)(2,1)S(1)} %collective-permute-done.7) | copy-start | bytes 393220
  81.5 15.2 %collective-permute-start.9 = (bf16[1,256,2,128]{1,3,2,0:T(8,128)(2,1)}, bf16[1,256,2,128]{1,3,2,0:T(8,128)(2,1)S(1)}, u32[]{:S(2)}, u32[]{:S(2)}) collective-permute-start(bf16[1,256,2,128]{1,3,2,0:T(8,128)(2,1)} %copy.222), channel_id=1, source_target_pairs={{0,8},{2,10},{4,12},{6,14},{8,16},{10,18},{12,20},{14,22},{16,24},... | collective-permute-start | bytes 393224 | tf_op jit(solution)/shard_map/ppermute | solution.py:13
  96.7 8.0 %collective-permute-start.8 = (bf16[1,256,2,128]{1,3,2,0:T(8,128)(2,1)}, bf16[1,256,2,128]{1,3,2,0:T(8,128)(2,1)S(1)}, u32[]{:S(2)}, u32[]{:S(2)}) collective-permute-start(bf16[1,256,2,128]{1,3,2,0:T(8,128)(2,1)} %copy.222), channel_id=1, source_target_pairs={{0,4},{2,6},{4,8},{6,10},{8,12},{10,14},{12,16},{14,18},{16,20},{1... | collective-permute-start | bytes 393224 | tf_op jit(solution)/shard_map/ppermute | solution.py:13
  147.4 11.9 %copy-start.20 = (bf16[1,256,2,128]{3,2,1,0:T(2,128)(2,1)S(1)}, bf16[1,256,2,128]{3,2,1,0:T(2,128)(2,1)}, u32[]{:S(2)}) copy-start(bf16[1,256,2,128]{3,2,1,0:T(2,128)(2,1)} %param.8) | copy-start | bytes 393220
  148.0 11.9 %copy-start.30 = (bf16[1,256,2,128]{3,1,2,0:T(8,128)(2,1)S(1)}, bf16[1,256,2,128]{3,1,2,0:T(8,128)(2,1)}, u32[]{:S(2)}) copy-start(bf16[1,256,2,128]{3,1,2,0:T(8,128)(2,1)} %copy-done.29) | copy-start | bytes 393220
  148.5 12.0 %copy-start.28 = (bf16[1,256,2,128]{3,1,2,0:T(8,128)(2,1)S(1)}, bf16[1,256,2,128]{3,1,2,0:T(8,128)(2,1)}, u32[]{:S(2)}) copy-start(bf16[1,256,2,128]{3,1,2,0:T(8,128)(2,1)} %copy-done.27) | copy-start | bytes 393220
  148.5 18.4 %collective-permute-start.14 = (bf16[1,256,2,128]{3,1,2,0:T(8,128)(2,1)S(1)}, bf16[1,256,2,128]{3,1,2,0:T(8,128)(2,1)S(1)}, u32[]{:S(2)}, u32[]{:S(2)}) collective-permute-start(bf16[1,256,2,128]{3,1,2,0:T(8,128)(2,1)S(1)} %fusion.91), channel_id=1, source_target_pairs={{4,0},{6,2},{8,4},{10,6},{12,8},{14,10},{16,12},{18,14},{20,16},{2... | collective-permute-start | bytes 393224 | tf_op jit(solution)/shard_map/ppermute | solution.py:13
  150.6 23.2 %collective-permute-start.21 = (bf16[1,256,2,128]{1,3,2,0:T(8,128)(2,1)S(1)}, bf16[1,256,2,128]{1,3,2,0:T(8,128)(2,1)S(1)}, u32[]{:S(2)}, u32[]{:S(2)}) collective-permute-start(bf16[1,256,2,128]{1,3,2,0:T(8,128)(2,1)S(1)} %copy-done.51), channel_id=1, source_target_pairs={{4,0},{6,2},{8,4},{10,6},{12,8},{14,10},{16,12},{18,14},{20,16},{2... | collective-permute-start | bytes 393224 | tf_op jit(solution)/shard_map/ppermute | solution.py:13
  153.3 22.3 %collective-permute-start.15 = (bf16[1,256,2,128]{3,1,2,0:T(8,128)(2,1)S(1)}, bf16[1,256,2,128]{3,1,2,0:T(8,128)(2,1)S(1)}, u32[]{:S(2)}, u32[]{:S(2)}) collective-permute-start(bf16[1,256,2,128]{3,1,2,0:T(8,128)(2,1)S(1)} %fusion.90), channel_id=1, source_target_pairs={{8,0},{10,2},{12,4},{14,6},{16,8},{18,10},{20,12},{22,14},{24,16},... | collective-permute-start | bytes 393224 | tf_op jit(solution)/shard_map/ppermute | solution.py:13
  155.3 21.7 %collective-permute-start.22 = (bf16[1,256,2,128]{1,3,2,0:T(8,128)(2,1)S(1)}, bf16[1,256,2,128]{1,3,2,0:T(8,128)(2,1)S(1)}, u32[]{:S(2)}, u32[]{:S(2)}) collective-permute-start(bf16[1,256,2,128]{1,3,2,0:T(8,128)(2,1)S(1)} %copy-done.50), channel_id=1, source_target_pairs={{8,0},{10,2},{12,4},{14,6},{16,8},{18,10},{20,12},{22,14},{24,16},... | collective-permute-start | bytes 393224 | tf_op jit(solution)/shard_map/ppermute | solution.py:13
  157.2 30.4 %collective-permute-start.16 = (bf16[1,256,2,128]{3,1,2,0:T(8,128)(2,1)S(1)}, bf16[1,256,2,128]{3,1,2,0:T(8,128)(2,1)S(1)}, u32[]{:S(2)}, u32[]{:S(2)}) collective-permute-start(bf16[1,256,2,128]{3,1,2,0:T(8,128)(2,1)S(1)} %fusion.89), channel_id=1, source_target_pairs={{16,0},{18,2},{20,4},{22,6},{24,8},{26,10},{28,12},{30,14},{32,16}... | collective-permute-start | bytes 393224 | tf_op jit(solution)/shard_map/ppermute | solution.py:13
  166.5 25.2 %copy-start.49 = (bf16[1,256,2,128]{1,3,2,0:T(8,128)(2,1)S(1)}, bf16[1,256,2,128]{1,3,2,0:T(8,128)(2,1)}, u32[]{:S(2)}) copy-start(bf16[1,256,2,128]{1,3,2,0:T(8,128)(2,1)} %fusion.81) | copy-start | bytes 393220
  166.5 27.2 %copy-start.48 = (bf16[1,256,2,128]{1,3,2,0:T(8,128)(2,1)S(1)}, bf16[1,256,2,128]{1,3,2,0:T(8,128)(2,1)}, u32[]{:S(2)}) copy-start(bf16[1,256,2,128]{1,3,2,0:T(8,128)(2,1)} %fusion.80) | copy-start | bytes 393220
  166.5 29.1 %copy-start.47 = (bf16[1,256,2,128]{1,3,2,0:T(8,128)(2,1)S(1)}, bf16[1,256,2,128]{1,3,2,0:T(8,128)(2,1)}, u32[]{:S(2)}) copy-start(bf16[1,256,2,128]{1,3,2,0:T(8,128)(2,1)} %fusion.79) | copy-start | bytes 393220
  166.5 30.4 %copy-start.46 = (bf16[1,256,2,128]{1,3,2,0:T(8,128)(2,1)S(1)}, bf16[1,256,2,128]{1,3,2,0:T(8,128)(2,1)}, u32[]{:S(2)}) copy-start(bf16[1,256,2,128]{1,3,2,0:T(8,128)(2,1)} %fusion.78) | copy-start | bytes 393220
  166.9 24.8 %collective-permute-start.17 = (bf16[1,256,2,128]{3,1,2,0:T(8,128)(2,1)S(1)}, bf16[1,256,2,128]{3,1,2,0:T(8,128)(2,1)S(1)}, u32[]{:S(2)}, u32[]{:S(2)}) collective-permute-start(bf16[1,256,2,128]{3,1,2,0:T(8,128)(2,1)S(1)} %fusion.88), channel_id=1, source_target_pairs={{32,0},{34,2},{36,4},{38,6},{40,8},{42,10},{44,12},{46,14},{48,16}... | collective-permute-start | bytes 393224 | tf_op jit(solution)/shard_map/ppermute | solution.py:13
  173.7 19.9 %collective-permute-start.18 = (bf16[1,256,2,128]{3,1,2,0:T(8,128)(2,1)S(1)}, bf16[1,256,2,128]{3,1,2,0:T(8,128)(2,1)S(1)}, u32[]{:S(2)}, u32[]{:S(2)}) collective-permute-start(bf16[1,256,2,128]{3,1,2,0:T(8,128)(2,1)S(1)} %fusion.87), channel_id=1, source_target_pairs={{64,0},{66,2},{68,4},{70,6},{72,8},{74,10},{76,12},{78,14},{80,16}... | collective-permute-start | bytes 393224 | tf_op jit(solution)/shard_map/ppermute | solution.py:13
  175.7 19.9 %collective-permute-start.19 = (bf16[1,256,2,128]{3,1,2,0:T(8,128)(2,1)S(1)}, bf16[1,256,2,128]{3,1,2,0:T(8,128)(2,1)S(1)}, u32[]{:S(2)}, u32[]{:S(2)}) collective-permute-start(bf16[1,256,2,128]{3,1,2,0:T(8,128)(2,1)S(1)} %fusion.86), channel_id=1, source_target_pairs={{128,0},{130,2},{132,4},{134,6},{136,8},{138,10},{140,12},{142,14}... | collective-permute-start | bytes 393224 | tf_op jit(solution)/shard_map/ppermute | solution.py:13
  177.0 19.9 %collective-permute-start.20 = (bf16[1,256,2,128]{3,1,2,0:T(8,128)(2,1)S(1)}, bf16[1,256,2,128]{3,1,2,0:T(8,128)(2,1)S(1)}, u32[]{:S(2)}, u32[]{:S(2)}) collective-permute-start(bf16[1,256,2,128]{3,1,2,0:T(8,128)(2,1)S(1)} %fusion.85), channel_id=1, source_target_pairs={{2,0},{4,2},{6,4},{8,6},{10,8},{12,10},{14,12},{16,14},{18,16},{20... | collective-permute-start | bytes 393224 | tf_op jit(solution)/shard_map/ppermute | solution.py:13
  187.6 13.3 %collective-permute-start.23 = (bf16[1,256,2,128]{1,3,2,0:T(8,128)(2,1)S(1)}, bf16[1,256,2,128]{1,3,2,0:T(8,128)(2,1)S(1)}, u32[]{:S(2)}, u32[]{:S(2)}) collective-permute-start(bf16[1,256,2,128]{1,3,2,0:T(8,128)(2,1)S(1)} %fusion.82), channel_id=1, source_target_pairs={{16,0},{18,2},{20,4},{22,6},{24,8},{26,10},{28,12},{30,14},{32,16}... | collective-permute-start | bytes 393224 | tf_op jit(solution)/shard_map/ppermute | solution.py:13
  191.7 14.4 %collective-permute-start.24 = (bf16[1,256,2,128]{1,3,2,0:T(8,128)(2,1)S(1)}, bf16[1,256,2,128]{1,3,2,0:T(8,128)(2,1)S(1)}, u32[]{:S(2)}, u32[]{:S(2)}) collective-permute-start(bf16[1,256,2,128]{1,3,2,0:T(8,128)(2,1)S(1)} %copy-done.49), channel_id=1, source_target_pairs={{32,0},{34,2},{36,4},{38,6},{40,8},{42,10},{44,12},{46,14},{48,16}... | collective-permute-start | bytes 393224 | tf_op jit(solution)/shard_map/ppermute | solution.py:13
  193.7 14.6 %collective-permute-start.25 = (bf16[1,256,2,128]{1,3,2,0:T(8,128)(2,1)S(1)}, bf16[1,256,2,128]{1,3,2,0:T(8,128)(2,1)S(1)}, u32[]{:S(2)}, u32[]{:S(2)}) collective-permute-start(bf16[1,256,2,128]{1,3,2,0:T(8,128)(2,1)S(1)} %copy-done.48), channel_id=1, source_target_pairs={{64,0},{66,2},{68,4},{70,6},{72,8},{74,10},{76,12},{78,14},{80,16}... | collective-permute-start | bytes 393224 | tf_op jit(solution)/shard_map/ppermute | solution.py:13
  195.6 18.6 %collective-permute-start.26 = (bf16[1,256,2,128]{1,3,2,0:T(8,128)(2,1)S(1)}, bf16[1,256,2,128]{1,3,2,0:T(8,128)(2,1)S(1)}, u32[]{:S(2)}, u32[]{:S(2)}) collective-permute-start(bf16[1,256,2,128]{1,3,2,0:T(8,128)(2,1)S(1)} %copy-done.47), channel_id=1, source_target_pairs={{128,0},{130,2},{132,4},{134,6},{136,8},{138,10},{140,12},{142,14}... | collective-permute-start | bytes 393224 | tf_op jit(solution)/shard_map/ppermute | solution.py:13
  196.9 17.3 %collective-permute-start.27 = (bf16[1,256,2,128]{1,3,2,0:T(8,128)(2,1)S(1)}, bf16[1,256,2,128]{1,3,2,0:T(8,128)(2,1)S(1)}, u32[]{:S(2)}, u32[]{:S(2)}) collective-permute-start(bf16[1,256,2,128]{1,3,2,0:T(8,128)(2,1)S(1)} %copy-done.46), channel_id=1, source_target_pairs={{2,0},{4,2},{6,4},{8,6},{10,8},{12,10},{14,12},{16,14},{18,16},{20... | collective-permute-start | bytes 393224 | tf_op jit(solution)/shard_map/ppermute | solution.py:13
  (34 other events, 102.5 us)
where the time goes:
time: 217 us; the launch traced here: 216 us
  starting transfers between devices  99.2 us (46%)
  waiting for transfers between devices  40.8 us (19%)
  matrix products  36 us (17%)
  local copies, waits for them, and re-layouts  17.3 us (8%)
  other arithmetic  10.1 us (5%)
  between operations  6.14 us (3%)
  blocking collectives  5.95 us (3%)
    ppermute x28, starting transfers between devices, passed_along(): lax.ppermute(value, axis, [(source, source + steps) for source in range(l...  99.2 us
    ppermute x28, waiting for transfers between devices, passed_along(): lax.ppermute(value, axis, [(source, source + steps) for source in range(l...  40.8 us
    dot_general x8, matrix products, per_device(): jnp.einsum('bhgus,buhgd->bshd', probabilities, grad_grouped, preferred_el...  11.6 us
    unnamed x113, local copies, waits for them, and re-layouts  10.4 us
    dot_general x8, matrix products, per_device(): jnp.einsum('bhgus,bshd->buhgd', probabilities, entry[1], preferred_elemen...  6.06 us
    psum x1, blocking collectives, per_device(): square_total = lax.psum(jnp.sum(attn_wide * attn_wide, axis=(2, 3)), 'head')  5.95 us
    dot_general x8, matrix products, per_device(): jnp.einsum('buhgd,bshd->bhgus', grad_grouped, value_block, preferred_elem...  5.82 us
    dot_general x8, matrix products, scores_of(): jnp.einsum('buhgd,bshd->bhgus', grouped, key_block, preferred_element_typ...  4.65 us
  transfers between devices with their start and end apart: 28, of which 11 were waited for; matrix products, arithmetic and copies ran while one was open for 10% of the time, Pallas kernels for 0%

commit v1 on v0

--- a/solution.py
+++ b/solution.py
@@ -3,6 +3,7 @@
 import jax.numpy as jnp
 from jax import lax
 from jax.sharding import PartitionSpec as P
+from jax.lax import all_gather
 
 epsilon = 1e-06
 
@@ -72,7 +73,12 @@
     )
     features = local_heads * lax.axis_size("head") * head_size
     attn_wide = attention.astype(jnp.float32)
-    square_total = lax.psum(jnp.sum(attn_wide * attn_wide, axis=(2, 3)), "head")
+
+    def check_the_layers_all(local_block):
+        outer = all_gather(local_block, "head").sum(axis=0)
+        return outer
+
+    square_total = check_the_layers_all(jnp.sum(attn_wide * attn_wide, axis=(2, 3)))
     inverse = lax.rsqrt(square_total / features + epsilon)
     normed = (norm_gain * attn_wide * inverse[..., None, None]).astype(jnp.bfloat16)
     scaled_grad = norm_gain * out_grad.astype(jnp.float32)

time: 217 us -> 224 us (1.032)
  blocking collectives: 5.95 us -> 10.8 us
    all_gather x0 -> x1, blocking collectives: none -> 4.79 us  [check_the_layers_all(): outer = all_gather(local_block, 'head').sum(axis=0)]
where the time goes in v1:
time: 224 us; the launch traced here: 223 us
  starting transfers between devices  101 us (45%)
  waiting for transfers between devices  40.5 us (18%)
  matrix products  36.6 us (16%)
  local copies, waits for them, and re-layouts  17.3 us (8%)
  other arithmetic  10.8 us (5%)
  blocking collectives  10.8 us (5%)
  between operations  6.23 us (3%)
    ppermute x28, starting transfers between devices, passed_along(): lax.ppermute(value, axis, [(source, source + steps) for source in range(l...  101 us
    ppermute x28, waiting for transfers between devices, passed_along(): lax.ppermute(value, axis, [(source, source + steps) for source in range(l...  40.5 us
    dot_general x8, matrix products, per_device(): jnp.einsum('bhgus,buhgd->bshd', probabilities, grad_grouped, preferred_el...  11.6 us
    unnamed x113, local copies, waits for them, and re-layouts  10.4 us
    dot_general x8, matrix products, per_device(): jnp.einsum('bhgus,bshd->buhgd', probabilities, entry[1], preferred_elemen...  6.63 us
    psum x1, blocking collectives, per_device(): dot_total = lax.psum(jnp.sum(scaled_grad * attn_wide, axis=(2, 3)), 'head')  6.02 us
    dot_general x8, matrix products, per_device(): jnp.einsum('buhgd,bshd->bhgus', grad_grouped, value_block, preferred_elem...  5.83 us
    all_gather x1, blocking collectives, check_the_layers_all(): outer = all_gather(local_block, 'head').sum(axis=0)  4.79 us
  transfers between devices with their start and end apart: 28, of which 11 were waited for; matrix products, arithmetic and copies ran while one was open for 10% of the time, Pallas kernels for 0%

profile of v1, /device:TPU:227, one launch (start us, length us, event | category | flops | bytes accessed | tf_op | source)
XLA Modules:
  0.0 223.0 jit_solution(9300986127555297348)
XLA Ops:
  0.7 1.7 copy.222
  2.4 3.7 %collective-permute-start.13 = (bf16[1,256,2,128]{1,3,2,0:T(8,128)(2,1)}, bf16[1,256,2,128]{1,3,2,0:T(8,128)(2,1)S(1)}, u32[]{:S(2)}, u32[]{:S(2)}) collective-permute-start(bf16[1,256,2,128]{1,3,2,0:T(8,128)(2,1)} %copy.222), channel_id=1, source_target_pairs={{0,128},{2,130},{4,132},{6,134},{8,136},{10,138},{12,140},{14,142}... | collective-permute-start | bytes 393224 | tf_op jit(solution)/shard_map/ppermute | solution.py:14
  6.2 1.9 collective-permute-start.12
  8.1 2.4 %collective-permute-start.11 = (bf16[1,256,2,128]{1,3,2,0:T(8,128)(2,1)}, bf16[1,256,2,128]{1,3,2,0:T(8,128)(2,1)S(1)}, u32[]{:S(2)}, u32[]{:S(2)}) collective-permute-start(bf16[1,256,2,128]{1,3,2,0:T(8,128)(2,1)} %copy.222), channel_id=1, source_target_pairs={{0,32},{2,34},{4,36},{6,38},{8,40},{10,42},{12,44},{14,46},{16,48}... | collective-permute-start | bytes 393224 | tf_op jit(solution)/shard_map/ppermute | solution.py:14
  10.5 5.2 %collective-permute-start.10 = (bf16[1,256,2,128]{1,3,2,0:T(8,128)(2,1)}, bf16[1,256,2,128]{1,3,2,0:T(8,128)(2,1)}, u32[]{:S(2)}, u32[]{:S(2)}) collective-permute-start(bf16[1,256,2,128]{1,3,2,0:T(8,128)(2,1)} %copy.222), channel_id=1, source_target_pairs={{0,16},{2,18},{4,20},{6,22},{8,24},{10,26},{12,28},{14,30},{16,32}... | collective-permute-start | bytes 393224 | tf_op jit(solution)/shard_map/ppermute | solution.py:14
  16.7 4.6 %collective-permute-start = (bf16[1,256,2,128]{3,1,2,0:T(8,128)(2,1)S(1)}, bf16[1,256,2,128]{3,1,2,0:T(8,128)(2,1)S(1)}, u32[]{:S(2)}, u32[]{:S(2)}) collective-permute-start(bf16[1,256,2,128]{3,1,2,0:T(8,128)(2,1)S(1)} %copy.206), channel_id=1, source_target_pairs={{0,2},{2,4},{4,6},{6,8},{8,10},{10,12},{12,14},{14,16},{16,18},{18... | collective-permute-start | bytes 393224 | tf_op jit(solution)/shard_map/ppermute | solution.py:14
  21.3 1.4 fusion.182
  28.1 2.5 %collective-permute-start.1 = (bf16[1,256,2,128]{3,1,2,0:T(8,128)(2,1)S(1)}, bf16[1,256,2,128]{3,1,2,0:T(8,128)(2,1)S(1)}, u32[]{:S(2)}, u32[]{:S(2)}) collective-permute-start(bf16[1,256,2,128]{3,1,2,0:T(8,128)(2,1)S(1)} %copy.206), channel_id=1, source_target_pairs={{0,4},{2,6},{4,8},{6,10},{8,12},{10,14},{12,16},{14,18},{16,20},{1... | collective-permute-start | bytes 393224 | tf_op jit(solution)/shard_map/ppermute | solution.py:14
  31.1 4.3 %collective-permute-done.1 = bf16[1,256,2,128]{3,1,2,0:T(8,128)(2,1)S(1)} collective-permute-done((bf16[1,256,2,128]{3,1,2,0:T(8,128)(2,1)S(1)}, bf16[1,256,2,128]{3,1,2,0:T(8,128)(2,1)S(1)}, u32[]{:S(2)}, u32[]{:S(2)}) %collective-permute-start.1) | collective-permute-done | bytes 131104 | tf_op jit(solution)/shard_map/ppermute | solution.py:14
  35.4 4.5 %collective-permute-start.2 = (bf16[1,256,2,128]{3,1,2,0:T(8,128)(2,1)S(1)}, bf16[1,256,2,128]{3,1,2,0:T(8,128)(2,1)S(1)}, u32[]{:S(2)}, u32[]{:S(2)}) collective-permute-start(bf16[1,256,2,128]{3,1,2,0:T(8,128)(2,1)S(1)} %copy.206), channel_id=1, source_target_pairs={{0,8},{2,10},{4,12},{6,14},{8,16},{10,18},{12,20},{14,22},{16,24},... | collective-permute-start | bytes 393224 | tf_op jit(solution)/shard_map/ppermute | solution.py:14
  40.4 2.0 collective-permute-done.2
  42.3 3.0 %collective-permute-start.3 = (bf16[1,256,2,128]{3,1,2,0:T(8,128)(2,1)S(1)}, bf16[1,256,2,128]{3,1,2,0:T(8,128)(2,1)S(1)}, u32[]{:S(2)}, u32[]{:S(2)}) collective-permute-start(bf16[1,256,2,128]{3,1,2,0:T(8,128)(2,1)S(1)} %copy.206), channel_id=1, source_target_pairs={{0,16},{2,18},{4,20},{6,22},{8,24},{10,26},{12,28},{14,30},{16,32}... | collective-permute-start | bytes 393224 | tf_op jit(solution)/shard_map/ppermute | solution.py:14
  45.8 5.2 %collective-permute-done.3 = bf16[1,256,2,128]{3,1,2,0:T(8,128)(2,1)S(1)} collective-permute-done((bf16[1,256,2,128]{3,1,2,0:T(8,128)(2,1)S(1)}, bf16[1,256,2,128]{3,1,2,0:T(8,128)(2,1)S(1)}, u32[]{:S(2)}, u32[]{:S(2)}) %collective-permute-start.3) | collective-permute-done | bytes 131104 | tf_op jit(solution)/shard_map/ppermute | solution.py:14
  51.0 1.9 collective-permute-start.4
  53.4 9.1 %collective-permute-done.4 = bf16[1,256,2,128]{3,1,2,0:T(8,128)(2,1)S(1)} collective-permute-done((bf16[1,256,2,128]{3,1,2,0:T(8,128)(2,1)S(1)}, bf16[1,256,2,128]{3,1,2,0:T(8,128)(2,1)S(1)}, u32[]{:S(2)}, u32[]{:S(2)}) %collective-permute-start.4) | collective-permute-done | bytes 131104 | tf_op jit(solution)/shard_map/ppermute | solution.py:14
  62.5 1.9 collective-permute-start.5
  64.9 3.3 %collective-permute-done.5 = bf16[1,256,2,128]{3,1,2,0:T(8,128)(2,1)S(1)} collective-permute-done((bf16[1,256,2,128]{3,1,2,0:T(8,128)(2,1)S(1)}, bf16[1,256,2,128]{3,1,2,0:T(8,128)(2,1)S(1)}, u32[]{:S(2)}, u32[]{:S(2)}) %collective-permute-start.5) | collective-permute-done | bytes 131104 | tf_op jit(solution)/shard_map/ppermute | solution.py:14
  70.0 1.4 collective-permute-done.6
  71.4 7.9 %collective-permute-start.7 = (bf16[1,256,2,128]{1,3,2,0:T(8,128)(2,1)}, bf16[1,256,2,128]{1,3,2,0:T(8,128)(2,1)S(1)}, u32[]{:S(2)}, u32[]{:S(2)}) collective-permute-start(bf16[1,256,2,128]{1,3,2,0:T(8,128)(2,1)} %copy.222), channel_id=1, source_target_pairs={{0,2},{2,4},{4,6},{6,8},{8,10},{10,12},{12,14},{14,16},{16,18},{18... | collective-permute-start | bytes 393224 | tf_op jit(solution)/shard_map/ppermute | solution.py:14
  82.9 11.9 %collective-permute-start.9 = (bf16[1,256,2,128]{1,3,2,0:T(8,128)(2,1)}, bf16[1,256,2,128]{1,3,2,0:T(8,128)(2,1)S(1)}, u32[]{:S(2)}, u32[]{:S(2)}) collective-permute-start(bf16[1,256,2,128]{1,3,2,0:T(8,128)(2,1)} %copy.222), channel_id=1, source_target_pairs={{0,8},{2,10},{4,12},{6,14},{8,16},{10,18},{12,20},{14,22},{16,24},... | collective-permute-start | bytes 393224 | tf_op jit(solution)/shard_map/ppermute | solution.py:14
  95.3 1.7 collective-permute-done.9
  97.1 4.2 %collective-permute-start.8 = (bf16[1,256,2,128]{1,3,2,0:T(8,128)(2,1)}, bf16[1,256,2,128]{1,3,2,0:T(8,128)(2,1)S(1)}, u32[]{:S(2)}, u32[]{:S(2)}) collective-permute-start(bf16[1,256,2,128]{1,3,2,0:T(8,128)(2,1)} %copy.222), channel_id=1, source_target_pairs={{0,4},{2,6},{4,8},{6,10},{8,12},{10,14},{12,16},{14,18},{16,20},{1... | collective-permute-start | bytes 393224 | tf_op jit(solution)/shard_map/ppermute | solution.py:14
  101.8 1.4 fusion.112
  105.6 2.2 fusion.100
  107.8 2.6 %copy.236 = f32[1,256,8,128]{3,2,1,0:T(8,128)} copy(f32[1,256,8,128]{1,3,2,0:T(8,128)} %bitcast.792) | data formatting | bytes 2097152 | tf_op jit(solution)/shard_map/convert_element_type | solution.py:75
  110.4 2.3 %multiply_reduce_fusion.1 = f32[256]{0:T(256)S(1)} fusion(f32[1,256,8,128]{3,2,1,0:T(8,128)} %copy.236, bf16[1,256,8,128]{3,2,1,0:T(8,128)(2,1)S(1)} %copy-done.19, f32[8,128]{1,0:T(8,128)S(1)} %copy-done.53), kind=kLoop, calls=%fused_computation.162 | loop fusion | flops 1048320 | bytes 1577984 | tf_op jit(solution)/shard_map/reduce_sum | solution.py:85
  112.7 6.0 %psum.7 = f32[1,256]{1,0:T(1,128)} all-reduce(f32[1,256]{1,0:T(1,128)S(1)} %bitcast.833), channel_id=1, replica_groups=mesh['seq'=128,'head'=2] {'head'}, use_global_device_ids=true, to_apply=%region_19.20 | all-reduce | flops 256 | bytes 2048 | tf_op jit(solution)/shard_map/psum | solution.py:85
  118.7 4.8 %all-gather.1 = f32[2,1,256]{2,1,0:T(1,128)S(1)} all-gather(f32[1,1,256]{2,1,0:T(1,128)} %bitcast.831), channel_id=2, replica_groups=mesh['seq'=128,'head'=2] {'head'}, dimensions={0}, use_global_device_ids=true | all-gather | bytes 3072 | tf_op jit(solution)/shard_map/all_gather | solution.py:78
  125.4 4.0 %multiply_reduce_fusion = (f32[256,8]{1,0:T(8,128)}, bf16[1,256,8,128]{3,2,1,0:T(8,128)(2,1)}, bf16[1,256,8,128]{3,2,1,0:T(8,128)(2,1)}) fusion(f32[1,256,8,128]{3,2,1,0:T(8,128)} %copy.236, f32[256]{0:T(256)S(1)} %bitcast.832, f32[256]{0:T(256)S(1)} %add_rsqrt_fusion, bf16[1,256,8,128]{3,2,1,0:T(8,128)(2,1)S(1)} %copy-done.19, f32[8,128]{1,0:T(8,128)S(1)} %copy-done.53), kind=kLoop, calls=%fused_computation.160 | loop fusion | flops 3143680 | bytes 2635776 | tf_op jit(solution)/shard_map/reduce_sum | solution.py:90
  129.5 1.3 copy.282
  130.8 2.9 %fusion.78 = bf16[1,256,2,128]{1,3,2,0:T(8,128)(2,1)} fusion(bf16[256,2,4,128]{0,3,2,1:T(8,128)(2,1)S(1)} %copy.282, f32[1,2,4,256,256]{3,4,2,1,0:T(8,128)} %copy-done.6, f32[2,4,256]{2,1,0:T(4,128)S(1)} %bitcast.776), kind=kOutput, calls=%fused_computation.136 | convolution fusion | flops 135331840 | bytes 2760704 | tf_op jit(solution)/shard_map/bhgus,buhgd->bshd/dot_general | solution.py:111
  133.7 2.9 %fusion.79 = bf16[1,256,2,128]{1,3,2,0:T(8,128)(2,1)} fusion(bf16[256,2,4,128]{0,3,2,1:T(8,128)(2,1)S(1)} %copy.282, f32[2,256,256,4]{2,1,3,0:T(8,128)} %copy-done.14, f32[2,4,256]{2,1,0:T(4,128)S(1)} %bitcast.777), kind=kOutput, calls=%fused_computation.137 | convolution fusion | flops 135331840 | bytes 2760704 | tf_op jit(solution)/shard_map/bhgus,buhgd->bshd/dot_general | solution.py:111
  141.3 1.6 copy.243
  149.9 1.7 fusion.46
  154.7 2.1 collective-permute-start.14
  156.9 2.7 %collective-permute-start.21 = (bf16[1,256,2,128]{1,3,2,0:T(8,128)(2,1)S(1)}, bf16[1,256,2,128]{1,3,2,0:T(8,128)(2,1)S(1)}, u32[]{:S(2)}, u32[]{:S(2)}) collective-permute-start(bf16[1,256,2,128]{1,3,2,0:T(8,128)(2,1)S(1)} %copy-done.51), channel_id=1, source_target_pairs={{4,0},{6,2},{8,4},{10,6},{12,8},{14,10},{16,12},{18,14},{20,16},{2... | collective-permute-start | bytes 393224 | tf_op jit(solution)/shard_map/ppermute | solution.py:14
  159.6 1.9 collective-permute-start.15
  161.5 1.9 collective-permute-start.22
  163.4 2.1 collective-permute-start.16
  173.2 6.8 %collective-permute-start.17 = (bf16[1,256,2,128]{3,1,2,0:T(8,128)(2,1)S(1)}, bf16[1,256,2,128]{3,1,2,0:T(8,128)(2,1)S(1)}, u32[]{:S(2)}, u32[]{:S(2)}) collective-permute-start(bf16[1,256,2,128]{3,1,2,0:T(8,128)(2,1)S(1)} %fusion.88), channel_id=1, source_target_pairs={{32,0},{34,2},{36,4},{38,6},{40,8},{42,10},{44,12},{46,14},{48,16}... | collective-permute-start | bytes 393224 | tf_op jit(solution)/shard_map/ppermute | solution.py:14
  179.9 1.9 collective-permute-start.18
  183.2 11.3 %collective-permute-start.20 = (bf16[1,256,2,128]{3,1,2,0:T(8,128)(2,1)S(1)}, bf16[1,256,2,128]{3,1,2,0:T(8,128)(2,1)S(1)}, u32[]{:S(2)}, u32[]{:S(2)}) collective-permute-start(bf16[1,256,2,128]{3,1,2,0:T(8,128)(2,1)S(1)} %fusion.85), channel_id=1, source_target_pairs={{2,0},{4,2},{6,4},{8,6},{10,8},{12,10},{14,12},{16,14},{18,16},{20... | collective-permute-start | bytes 393224 | tf_op jit(solution)/shard_map/ppermute | solution.py:14
  195.0 4.3 %collective-permute-start.23 = (bf16[1,256,2,128]{1,3,2,0:T(8,128)(2,1)S(1)}, bf16[1,256,2,128]{1,3,2,0:T(8,128)(2,1)S(1)}, u32[]{:S(2)}, u32[]{:S(2)}) collective-permute-start(bf16[1,256,2,128]{1,3,2,0:T(8,128)(2,1)S(1)} %fusion.82), channel_id=1, source_target_pairs={{16,0},{18,2},{20,4},{22,6},{24,8},{26,10},{28,12},{30,14},{32,16}... | collective-permute-start | bytes 393224 | tf_op jit(solution)/shard_map/ppermute | solution.py:14
  199.3 1.9 collective-permute-start.24
  201.3 1.9 collective-permute-start.25
  204.5 2.2 collective-permute-start.27
  208.3 5.2 %collective-permute-done.24 = bf16[1,256,2,128]{1,3,2,0:T(8,128)(2,1)S(1)} collective-permute-done((bf16[1,256,2,128]{1,3,2,0:T(8,128)(2,1)S(1)}, bf16[1,256,2,128]{1,3,2,0:T(8,128)(2,1)S(1)}, u32[]{:S(2)}, u32[]{:S(2)}) %collective-permute-start.24) | collective-permute-done | bytes 131104 | tf_op jit(solution)/shard_map/ppermute | solution.py:14
  214.3 7.3 %collective-permute-done.26 = bf16[1,256,2,128]{1,3,2,0:T(8,128)(2,1)S(1)} collective-permute-done((bf16[1,256,2,128]{1,3,2,0:T(8,128)(2,1)S(1)}, bf16[1,256,2,128]{1,3,2,0:T(8,128)(2,1)S(1)}, u32[]{:S(2)}, u32[]{:S(2)}) %collective-permute-start.26) | collective-permute-done | bytes 131104 | tf_op jit(solution)/shard_map/ppermute | solution.py:14
  (190 shorter events, 43.7 us)
Async XLA Ops:
  0.6 20.7 %copy-start = (bf16[1,256,8,128]{3,2,1,0:T(8,128)(2,1)S(1)}, bf16[1,256,8,128]{3,2,1,0:T(8,128)(2,1)}, u32[]{:S(2)}) copy-start(bf16[1,256,8,128]{3,2,1,0:T(8,128)(2,1)} %param.7) | copy-start | bytes 1572868
  0.6 27.2 %copy-start.33 = (bf16[1,256,2,128]{3,2,1,0:T(2,128)(2,1)S(1)}, bf16[1,256,2,128]{3,2,1,0:T(2,128)(2,1)}, u32[]{:S(2)}) copy-start(bf16[1,256,2,128]{3,2,1,0:T(2,128)(2,1)} %param.9) | copy-start | bytes 393220
  0.7 22.1 %copy-start.52 = (s32[1,1,6]{2,1,0:T(1,128)S(1)}, s32[1,1,6]{2,1,0:T(1,128)}, u32[]{:S(2)}) copy-start(s32[1,1,6]{2,1,0:T(1,128)} %param.13) | copy-start | bytes 76
  2.4 101.9 %collective-permute-start.13 = (bf16[1,256,2,128]{1,3,2,0:T(8,128)(2,1)}, bf16[1,256,2,128]{1,3,2,0:T(8,128)(2,1)S(1)}, u32[]{:S(2)}, u32[]{:S(2)}) collective-permute-start(bf16[1,256,2,128]{1,3,2,0:T(8,128)(2,1)} %copy.222), channel_id=1, source_target_pairs={{0,128},{2,130},{4,132},{6,134},{8,136},{10,138},{12,140},{14,142}... | collective-permute-start | bytes 393224 | tf_op jit(solution)/shard_map/ppermute | solution.py:14
  6.2 97.6 %collective-permute-start.12 = (bf16[1,256,2,128]{1,3,2,0:T(8,128)(2,1)}, bf16[1,256,2,128]{1,3,2,0:T(8,128)(2,1)S(1)}, u32[]{:S(2)}, u32[]{:S(2)}) collective-permute-start(bf16[1,256,2,128]{1,3,2,0:T(8,128)(2,1)} %copy.222), channel_id=1, source_target_pairs={{0,64},{2,66},{4,68},{6,70},{8,72},{10,74},{12,76},{14,78},{16,80}... | collective-permute-start | bytes 393224 | tf_op jit(solution)/shard_map/ppermute | solution.py:14
  8.1 95.1 %collective-permute-start.11 = (bf16[1,256,2,128]{1,3,2,0:T(8,128)(2,1)}, bf16[1,256,2,128]{1,3,2,0:T(8,128)(2,1)S(1)}, u32[]{:S(2)}, u32[]{:S(2)}) collective-permute-start(bf16[1,256,2,128]{1,3,2,0:T(8,128)(2,1)} %copy.222), channel_id=1, source_target_pairs={{0,32},{2,34},{4,36},{6,38},{8,40},{10,42},{12,44},{14,46},{16,48}... | collective-permute-start | bytes 393224 | tf_op jit(solution)/shard_map/ppermute | solution.py:14
  10.5 91.2 %collective-permute-start.10 = (bf16[1,256,2,128]{1,3,2,0:T(8,128)(2,1)}, bf16[1,256,2,128]{1,3,2,0:T(8,128)(2,1)}, u32[]{:S(2)}, u32[]{:S(2)}) collective-permute-start(bf16[1,256,2,128]{1,3,2,0:T(8,128)(2,1)} %copy.222), channel_id=1, source_target_pairs={{0,16},{2,18},{4,20},{6,22},{8,24},{10,26},{12,28},{14,30},{16,32}... | collective-permute-start | bytes 393224 | tf_op jit(solution)/shard_map/ppermute | solution.py:14
  16.7 11.4 %collective-permute-start = (bf16[1,256,2,128]{3,1,2,0:T(8,128)(2,1)S(1)}, bf16[1,256,2,128]{3,1,2,0:T(8,128)(2,1)S(1)}, u32[]{:S(2)}, u32[]{:S(2)}) collective-permute-start(bf16[1,256,2,128]{3,1,2,0:T(8,128)(2,1)S(1)} %copy.206), channel_id=1, source_target_pairs={{0,2},{2,4},{4,6},{6,8},{8,10},{10,12},{12,14},{14,16},{16,18},{18... | collective-permute-start | bytes 393224 | tf_op jit(solution)/shard_map/ppermute | solution.py:14
  22.8 57.1 %copy-start.44 = (f32[2,4,256]{2,1,0:T(4,128)}, f32[2,4,256]{2,1,0:T(4,128)S(1)}, u32[]{:S(2)}) copy-start(f32[2,4,256]{2,1,0:T(4,128)S(1)} %get-tuple-element.44) | copy-start | bytes 24580
  28.1 7.3 %collective-permute-start.1 = (bf16[1,256,2,128]{3,1,2,0:T(8,128)(2,1)S(1)}, bf16[1,256,2,128]{3,1,2,0:T(8,128)(2,1)S(1)}, u32[]{:S(2)}, u32[]{:S(2)}) collective-permute-start(bf16[1,256,2,128]{3,1,2,0:T(8,128)(2,1)S(1)} %copy.206), channel_id=1, source_target_pairs={{0,4},{2,6},{4,8},{6,10},{8,12},{10,14},{12,16},{14,18},{16,20},{1... | collective-permute-start | bytes 393224 | tf_op jit(solution)/shard_map/ppermute | solution.py:14
  31.1 63.7 %copy-start.6 = (f32[1,2,4,256,256]{3,4,2,1,0:T(8,128)}, f32[1,2,4,256,256]{3,4,2,1,0:T(8,128)S(1)}, u32[]{:S(2)}) copy-start(f32[1,2,4,256,256]{3,4,2,1,0:T(8,128)S(1)} %get-tuple-element.47) | copy-start | bytes 6291460
  35.4 7.0 %collective-permute-start.2 = (bf16[1,256,2,128]{3,1,2,0:T(8,128)(2,1)S(1)}, bf16[1,256,2,128]{3,1,2,0:T(8,128)(2,1)S(1)}, u32[]{:S(2)}, u32[]{:S(2)}) collective-permute-start(bf16[1,256,2,128]{3,1,2,0:T(8,128)(2,1)S(1)} %copy.206), channel_id=1, source_target_pairs={{0,8},{2,10},{4,12},{6,14},{8,16},{10,18},{12,20},{14,22},{16,24},... | collective-permute-start | bytes 393224 | tf_op jit(solution)/shard_map/ppermute | solution.py:14
  40.4 64.4 %copy-start.16 = (f32[2,256,256,4]{2,1,3,0:T(8,128)}, f32[2,256,256,4]{2,1,3,0:T(8,128)S(1)}, u32[]{:S(2)}) copy-start(f32[2,256,256,4]{2,1,3,0:T(8,128)S(1)} %get-tuple-element.43) | copy-start | bytes 6291460
  42.3 8.7 %collective-permute-start.3 = (bf16[1,256,2,128]{3,1,2,0:T(8,128)(2,1)S(1)}, bf16[1,256,2,128]{3,1,2,0:T(8,128)(2,1)S(1)}, u32[]{:S(2)}, u32[]{:S(2)}) collective-permute-start(bf16[1,256,2,128]{3,1,2,0:T(8,128)(2,1)S(1)} %copy.206), channel_id=1, source_target_pairs={{0,16},{2,18},{4,20},{6,22},{8,24},{10,26},{12,28},{14,30},{16,32}... | collective-permute-start | bytes 393224 | tf_op jit(solution)/shard_map/ppermute | solution.py:14
  45.8 55.4 %copy-start.8 = (f32[2,256,256,4]{2,1,3,0:T(8,128)}, f32[2,256,256,4]{2,1,3,0:T(8,128)S(1)}, u32[]{:S(2)}) copy-start(f32[2,256,256,4]{2,1,3,0:T(8,128)S(1)} %get-tuple-element.41) | copy-start | bytes 6291460
  51.0 13.9 %copy-start.23 = (bf16[1,256,2,128]{3,1,2,0:T(8,128)(2,1)}, bf16[1,256,2,128]{3,1,2,0:T(8,128)(2,1)S(1)}, u32[]{:S(2)}) copy-start(bf16[1,256,2,128]{3,1,2,0:T(8,128)(2,1)S(1)} %collective-permute-done.3) | copy-start | bytes 393220
  51.0 11.5 %collective-permute-start.4 = (bf16[1,256,2,128]{3,1,2,0:T(8,128)(2,1)S(1)}, bf16[1,256,2,128]{3,1,2,0:T(8,128)(2,1)S(1)}, u32[]{:S(2)}, u32[]{:S(2)}) collective-permute-start(bf16[1,256,2,128]{3,1,2,0:T(8,128)(2,1)S(1)} %copy.206), channel_id=1, source_target_pairs={{0,32},{2,34},{4,36},{6,38},{8,40},{10,42},{12,44},{14,46},{16,48}... | collective-permute-start | bytes 393224 | tf_op jit(solution)/shard_map/ppermute | solution.py:14
  53.4 48.4 %copy-start.1 = (f32[2,256,256,4]{2,1,3,0:T(8,128)}, f32[2,256,256,4]{2,1,3,0:T(8,128)S(1)}, u32[]{:S(2)}) copy-start(f32[2,256,256,4]{2,1,3,0:T(8,128)S(1)} %get-tuple-element.39) | copy-start | bytes 6291460
  62.5 5.7 %collective-permute-start.5 = (bf16[1,256,2,128]{3,1,2,0:T(8,128)(2,1)S(1)}, bf16[1,256,2,128]{3,1,2,0:T(8,128)(2,1)S(1)}, u32[]{:S(2)}, u32[]{:S(2)}) collective-permute-start(bf16[1,256,2,128]{3,1,2,0:T(8,128)(2,1)S(1)} %copy.206), channel_id=1, source_target_pairs={{0,64},{2,66},{4,68},{6,70},{8,72},{10,74},{12,76},{14,78},{16,80}... | collective-permute-start | bytes 393224 | tf_op jit(solution)/shard_map/ppermute | solution.py:14
  64.9 38.3 %copy-start.3 = (f32[2,256,256,4]{2,1,3,0:T(8,128)}, f32[2,256,256,4]{2,1,3,0:T(8,128)S(1)}, u32[]{:S(2)}) copy-start(f32[2,256,256,4]{2,1,3,0:T(8,128)S(1)} %get-tuple-element.37) | copy-start | bytes 6291460
  68.2 3.2 %collective-permute-start.6 = (bf16[1,256,2,128]{3,1,2,0:T(8,128)(2,1)S(1)}, bf16[1,256,2,128]{3,1,2,0:T(8,128)(2,1)S(1)}, u32[]{:S(2)}, u32[]{:S(2)}) collective-permute-start(bf16[1,256,2,128]{3,1,2,0:T(8,128)(2,1)S(1)} %copy.206), channel_id=1, source_target_pairs={{0,128},{2,130},{4,132},{6,134},{8,136},{10,138},{12,140},{14,142}... | collective-permute-start | bytes 393224 | tf_op jit(solution)/shard_map/ppermute | solution.py:14
  70.0 33.8 %copy-start.11 = (f32[2,256,256,4]{2,1,3,0:T(8,128)}, f32[2,256,256,4]{2,1,3,0:T(8,128)S(1)}, u32[]{:S(2)}) copy-start(f32[2,256,256,4]{2,1,3,0:T(8,128)S(1)} %get-tuple-element.35) | copy-start | bytes 6291460
  71.4 11.5 %collective-permute-start.7 = (bf16[1,256,2,128]{1,3,2,0:T(8,128)(2,1)}, bf16[1,256,2,128]{1,3,2,0:T(8,128)(2,1)S(1)}, u32[]{:S(2)}, u32[]{:S(2)}) collective-permute-start(bf16[1,256,2,128]{1,3,2,0:T(8,128)(2,1)} %copy.222), channel_id=1, source_target_pairs={{0,2},{2,4},{4,6},{6,8},{8,10},{10,12},{12,14},{14,16},{16,18},{18... | collective-permute-start | bytes 393224 | tf_op jit(solution)/shard_map/ppermute | solution.py:14
  79.8 24.5 %copy-start.14 = (f32[2,256,256,4]{2,1,3,0:T(8,128)}, f32[2,256,256,4]{2,1,3,0:T(8,128)S(1)}, u32[]{:S(2)}) copy-start(f32[2,256,256,4]{2,1,3,0:T(8,128)S(1)} %get-tuple-element.33) | copy-start | bytes 6291460
  82.9 12.5 %copy-start.40 = (bf16[1,256,2,128]{1,3,2,0:T(8,128)(2,1)}, bf16[1,256,2,128]{1,3,2,0:T(8,128)(2,1)S(1)}, u32[]{:S(2)}) copy-start(bf16[1,256,2,128]{1,3,2,0:T(8,128)(2,1)S(1)} %collective-permute-done.7) | copy-start | bytes 393220
  82.9 14.2 %collective-permute-start.9 = (bf16[1,256,2,128]{1,3,2,0:T(8,128)(2,1)}, bf16[1,256,2,128]{1,3,2,0:T(8,128)(2,1)S(1)}, u32[]{:S(2)}, u32[]{:S(2)}) collective-permute-start(bf16[1,256,2,128]{1,3,2,0:T(8,128)(2,1)} %copy.222), channel_id=1, source_target_pairs={{0,8},{2,10},{4,12},{6,14},{8,16},{10,18},{12,20},{14,22},{16,24},... | collective-permute-start | bytes 393224 | tf_op jit(solution)/shard_map/ppermute | solution.py:14
  97.1 7.8 %collective-permute-start.8 = (bf16[1,256,2,128]{1,3,2,0:T(8,128)(2,1)}, bf16[1,256,2,128]{1,3,2,0:T(8,128)(2,1)S(1)}, u32[]{:S(2)}, u32[]{:S(2)}) collective-permute-start(bf16[1,256,2,128]{1,3,2,0:T(8,128)(2,1)} %copy.222), channel_id=1, source_target_pairs={{0,4},{2,6},{4,8},{6,10},{8,12},{10,14},{12,16},{14,18},{16,20},{1... | collective-permute-start | bytes 393224 | tf_op jit(solution)/shard_map/ppermute | solution.py:14
  153.6 11.9 %copy-start.20 = (bf16[1,256,2,128]{3,2,1,0:T(2,128)(2,1)S(1)}, bf16[1,256,2,128]{3,2,1,0:T(2,128)(2,1)}, u32[]{:S(2)}) copy-start(bf16[1,256,2,128]{3,2,1,0:T(2,128)(2,1)} %param.8) | copy-start | bytes 393220
  154.3 11.9 %copy-start.30 = (bf16[1,256,2,128]{3,1,2,0:T(8,128)(2,1)S(1)}, bf16[1,256,2,128]{3,1,2,0:T(8,128)(2,1)}, u32[]{:S(2)}) copy-start(bf16[1,256,2,128]{3,1,2,0:T(8,128)(2,1)} %copy-done.29) | copy-start | bytes 393220
  154.7 12.0 %copy-start.28 = (bf16[1,256,2,128]{3,1,2,0:T(8,128)(2,1)S(1)}, bf16[1,256,2,128]{3,1,2,0:T(8,128)(2,1)}, u32[]{:S(2)}) copy-start(bf16[1,256,2,128]{3,1,2,0:T(8,128)(2,1)} %copy-done.27) | copy-start | bytes 393220
  154.7 18.5 %collective-permute-start.14 = (bf16[1,256,2,128]{3,1,2,0:T(8,128)(2,1)S(1)}, bf16[1,256,2,128]{3,1,2,0:T(8,128)(2,1)S(1)}, u32[]{:S(2)}, u32[]{:S(2)}) collective-permute-start(bf16[1,256,2,128]{3,1,2,0:T(8,128)(2,1)S(1)} %fusion.91), channel_id=1, source_target_pairs={{4,0},{6,2},{8,4},{10,6},{12,8},{14,10},{16,12},{18,14},{20,16},{2... | collective-permute-start | bytes 393224 | tf_op jit(solution)/shard_map/ppermute | solution.py:14
  156.9 23.1 %collective-permute-start.21 = (bf16[1,256,2,128]{1,3,2,0:T(8,128)(2,1)S(1)}, bf16[1,256,2,128]{1,3,2,0:T(8,128)(2,1)S(1)}, u32[]{:S(2)}, u32[]{:S(2)}) collective-permute-start(bf16[1,256,2,128]{1,3,2,0:T(8,128)(2,1)S(1)} %copy-done.51), channel_id=1, source_target_pairs={{4,0},{6,2},{8,4},{10,6},{12,8},{14,10},{16,12},{18,14},{20,16},{2... | collective-permute-start | bytes 393224 | tf_op jit(solution)/shard_map/ppermute | solution.py:14
  159.6 22.3 %collective-permute-start.15 = (bf16[1,256,2,128]{3,1,2,0:T(8,128)(2,1)S(1)}, bf16[1,256,2,128]{3,1,2,0:T(8,128)(2,1)S(1)}, u32[]{:S(2)}, u32[]{:S(2)}) collective-permute-start(bf16[1,256,2,128]{3,1,2,0:T(8,128)(2,1)S(1)} %fusion.90), channel_id=1, source_target_pairs={{8,0},{10,2},{12,4},{14,6},{16,8},{18,10},{20,12},{22,14},{24,16},... | collective-permute-start | bytes 393224 | tf_op jit(solution)/shard_map/ppermute | solution.py:14
  161.5 21.7 %collective-permute-start.22 = (bf16[1,256,2,128]{1,3,2,0:T(8,128)(2,1)S(1)}, bf16[1,256,2,128]{1,3,2,0:T(8,128)(2,1)S(1)}, u32[]{:S(2)}, u32[]{:S(2)}) collective-permute-start(bf16[1,256,2,128]{1,3,2,0:T(8,128)(2,1)S(1)} %copy-done.50), channel_id=1, source_target_pairs={{8,0},{10,2},{12,4},{14,6},{16,8},{18,10},{20,12},{22,14},{24,16},... | collective-permute-start | bytes 393224 | tf_op jit(solution)/shard_map/ppermute | solution.py:14
  163.4 31.5 %collective-permute-start.16 = (bf16[1,256,2,128]{3,1,2,0:T(8,128)(2,1)S(1)}, bf16[1,256,2,128]{3,1,2,0:T(8,128)(2,1)S(1)}, u32[]{:S(2)}, u32[]{:S(2)}) collective-permute-start(bf16[1,256,2,128]{3,1,2,0:T(8,128)(2,1)S(1)} %fusion.89), channel_id=1, source_target_pairs={{16,0},{18,2},{20,4},{22,6},{24,8},{26,10},{28,12},{30,14},{32,16}... | collective-permute-start | bytes 393224 | tf_op jit(solution)/shard_map/ppermute | solution.py:14
  172.7 26.6 %copy-start.49 = (bf16[1,256,2,128]{1,3,2,0:T(8,128)(2,1)S(1)}, bf16[1,256,2,128]{1,3,2,0:T(8,128)(2,1)}, u32[]{:S(2)}) copy-start(bf16[1,256,2,128]{1,3,2,0:T(8,128)(2,1)} %fusion.81) | copy-start | bytes 393220
  172.7 28.6 %copy-start.48 = (bf16[1,256,2,128]{1,3,2,0:T(8,128)(2,1)S(1)}, bf16[1,256,2,128]{1,3,2,0:T(8,128)(2,1)}, u32[]{:S(2)}) copy-start(bf16[1,256,2,128]{1,3,2,0:T(8,128)(2,1)} %fusion.80) | copy-start | bytes 393220
  172.7 30.5 %copy-start.47 = (bf16[1,256,2,128]{1,3,2,0:T(8,128)(2,1)S(1)}, bf16[1,256,2,128]{1,3,2,0:T(8,128)(2,1)}, u32[]{:S(2)}) copy-start(bf16[1,256,2,128]{1,3,2,0:T(8,128)(2,1)} %fusion.79) | copy-start | bytes 393220
  172.7 31.8 %copy-start.46 = (bf16[1,256,2,128]{1,3,2,0:T(8,128)(2,1)S(1)}, bf16[1,256,2,128]{1,3,2,0:T(8,128)(2,1)}, u32[]{:S(2)}) copy-start(bf16[1,256,2,128]{1,3,2,0:T(8,128)(2,1)} %fusion.78) | copy-start | bytes 393220
  173.2 26.1 %collective-permute-start.17 = (bf16[1,256,2,128]{3,1,2,0:T(8,128)(2,1)S(1)}, bf16[1,256,2,128]{3,1,2,0:T(8,128)(2,1)S(1)}, u32[]{:S(2)}, u32[]{:S(2)}) collective-permute-start(bf16[1,256,2,128]{3,1,2,0:T(8,128)(2,1)S(1)} %fusion.88), channel_id=1, source_target_pairs={{32,0},{34,2},{36,4},{38,6},{40,8},{42,10},{44,12},{46,14},{48,16}... | collective-permute-start | bytes 393224 | tf_op jit(solution)/shard_map/ppermute | solution.py:14
  179.9 21.3 %collective-permute-start.18 = (bf16[1,256,2,128]{3,1,2,0:T(8,128)(2,1)S(1)}, bf16[1,256,2,128]{3,1,2,0:T(8,128)(2,1)S(1)}, u32[]{:S(2)}, u32[]{:S(2)}) collective-permute-start(bf16[1,256,2,128]{3,1,2,0:T(8,128)(2,1)S(1)} %fusion.87), channel_id=1, source_target_pairs={{64,0},{66,2},{68,4},{70,6},{72,8},{74,10},{76,12},{78,14},{80,16}... | collective-permute-start | bytes 393224 | tf_op jit(solution)/shard_map/ppermute | solution.py:14
  181.9 21.3 %collective-permute-start.19 = (bf16[1,256,2,128]{3,1,2,0:T(8,128)(2,1)S(1)}, bf16[1,256,2,128]{3,1,2,0:T(8,128)(2,1)S(1)}, u32[]{:S(2)}, u32[]{:S(2)}) collective-permute-start(bf16[1,256,2,128]{3,1,2,0:T(8,128)(2,1)S(1)} %fusion.86), channel_id=1, source_target_pairs={{128,0},{130,2},{132,4},{134,6},{136,8},{138,10},{140,12},{142,14}... | collective-permute-start | bytes 393224 | tf_op jit(solution)/shard_map/ppermute | solution.py:14
  183.2 21.3 %collective-permute-start.20 = (bf16[1,256,2,128]{3,1,2,0:T(8,128)(2,1)S(1)}, bf16[1,256,2,128]{3,1,2,0:T(8,128)(2,1)S(1)}, u32[]{:S(2)}, u32[]{:S(2)}) collective-permute-start(bf16[1,256,2,128]{3,1,2,0:T(8,128)(2,1)S(1)} %fusion.85), channel_id=1, source_target_pairs={{2,0},{4,2},{6,4},{8,6},{10,8},{12,10},{14,12},{16,14},{18,16},{20... | collective-permute-start | bytes 393224 | tf_op jit(solution)/shard_map/ppermute | solution.py:14
  195.0 13.3 %collective-permute-start.23 = (bf16[1,256,2,128]{1,3,2,0:T(8,128)(2,1)S(1)}, bf16[1,256,2,128]{1,3,2,0:T(8,128)(2,1)S(1)}, u32[]{:S(2)}, u32[]{:S(2)}) collective-permute-start(bf16[1,256,2,128]{1,3,2,0:T(8,128)(2,1)S(1)} %fusion.82), channel_id=1, source_target_pairs={{16,0},{18,2},{20,4},{22,6},{24,8},{26,10},{28,12},{30,14},{32,16}... | collective-permute-start | bytes 393224 | tf_op jit(solution)/shard_map/ppermute | solution.py:14
  199.3 14.2 %collective-permute-start.24 = (bf16[1,256,2,128]{1,3,2,0:T(8,128)(2,1)S(1)}, bf16[1,256,2,128]{1,3,2,0:T(8,128)(2,1)S(1)}, u32[]{:S(2)}, u32[]{:S(2)}) collective-permute-start(bf16[1,256,2,128]{1,3,2,0:T(8,128)(2,1)S(1)} %copy-done.49), channel_id=1, source_target_pairs={{32,0},{34,2},{36,4},{38,6},{40,8},{42,10},{44,12},{46,14},{48,16}... | collective-permute-start | bytes 393224 | tf_op jit(solution)/shard_map/ppermute | solution.py:14
  201.3 13.0 %collective-permute-start.25 = (bf16[1,256,2,128]{1,3,2,0:T(8,128)(2,1)S(1)}, bf16[1,256,2,128]{1,3,2,0:T(8,128)(2,1)S(1)}, u32[]{:S(2)}, u32[]{:S(2)}) collective-permute-start(bf16[1,256,2,128]{1,3,2,0:T(8,128)(2,1)S(1)} %copy-done.48), channel_id=1, source_target_pairs={{64,0},{66,2},{68,4},{70,6},{72,8},{74,10},{76,12},{78,14},{80,16}... | collective-permute-start | bytes 393224 | tf_op jit(solution)/shard_map/ppermute | solution.py:14
  203.2 18.4 %collective-permute-start.26 = (bf16[1,256,2,128]{1,3,2,0:T(8,128)(2,1)S(1)}, bf16[1,256,2,128]{1,3,2,0:T(8,128)(2,1)S(1)}, u32[]{:S(2)}, u32[]{:S(2)}) collective-permute-start(bf16[1,256,2,128]{1,3,2,0:T(8,128)(2,1)S(1)} %copy-done.47), channel_id=1, source_target_pairs={{128,0},{130,2},{132,4},{134,6},{136,8},{138,10},{140,12},{142,14}... | collective-permute-start | bytes 393224 | tf_op jit(solution)/shard_map/ppermute | solution.py:14
  204.5 17.1 %collective-permute-start.27 = (bf16[1,256,2,128]{1,3,2,0:T(8,128)(2,1)S(1)}, bf16[1,256,2,128]{1,3,2,0:T(8,128)(2,1)S(1)}, u32[]{:S(2)}, u32[]{:S(2)}) collective-permute-start(bf16[1,256,2,128]{1,3,2,0:T(8,128)(2,1)S(1)} %copy-done.46), channel_id=1, source_target_pairs={{2,0},{4,2},{6,4},{8,6},{10,8},{12,10},{14,12},{16,14},{18,16},{20... | collective-permute-start | bytes 393224 | tf_op jit(solution)/shard_map/ppermute | solution.py:14
  (34 other events, 104.7 us)
